TPU v7x, 256 devices: a whole 4x4x8 slice. The times are simulated.
256 devices in a mesh: dom: 32 (over z_lo, y, x), ch: 8 (over z_hi, core).
Axes of the slice: x: 4, y: 4, z: 8 (z_hi: 4, z_lo: 2; z = z_hi * 2 + z_lo), core: 2. Of those that a mesh axis runs over, the one named last changes fastest.
Arguments:
- node_feats: bfloat16 [512, 24576], P('ch', 'dom'), may hold values from -6 to 6
- edge_feats: bfloat16 [512, 32768], P('ch', 'dom'), may hold values from -6 to 6
- send_rows: int32 [32768], P('dom'), may hold values from 0 to 767
- edge_src: int32 [32768], P('dom'), may hold values from 0 to 1791
- edge_dst: int32 [32768], P('dom'), may hold values from 0 to 767
- w_edge_in: bfloat16 [2, 3, 512, 512], P(None, None, None, 'ch'), may hold values from -0.15625 to 0.15625
- w_edge_out: bfloat16 [2, 512, 512], P(None, 'ch'), may hold values from -0.25 to 0.25
- w_node_in: bfloat16 [2, 2, 512, 512], P(None, None, None, 'ch'), may hold values from -0.1875 to 0.1875
- w_node_out: bfloat16 [2, 512, 512], P(None, 'ch'), may hold values from -0.25 to 0.25
Outputs:
- nodes_out: bfloat16 [512, 24576], P('ch', 'dom')
- edges_out: bfloat16 [512, 32768], P('ch', 'dom')
All inputs are finite; a program needn't handle non-finite values.
Results may differ from a plain program's by a relative error of at most 0.0085.
Values may be sent and summed in bfloat16 or wider, within the bound.
No kernel may reach another device: no remote copies, remote signals or barrier semaphores. Data moves between devices by JAX's collectives and lax.ppermute only.
A program may use at most 64 MiB of HBM per device.

v0:
```python
import jax
import jax.numpy as jnp
from jax import lax
from jax.sharding import PartitionSpec as P

LATENT = 512
SLOTS = 32
LAYERS = 2


def finish(hidden, weight_out, residual):
    summed = lax.psum_scatter(
        lax.dot_general(
            weight_out, hidden, (((0,), (0,)), ((), ())), preferred_element_type=jnp.float32
        ),
        "ch",
        scatter_dimension=0,
        tiled=True,
    )
    total, squares = lax.psum((jnp.sum(summed, axis=0), jnp.sum(summed * summed, axis=0)), "ch")
    mean = total / LATENT
    var = squares / LATENT - mean * mean
    normed = (summed - mean) * lax.rsqrt(var + 1e-05)
    return (residual.astype(jnp.float32) + normed).astype(jnp.bfloat16)


def edge_hidden(stacked, weight_in):
    return jnp.einsum(
        "akh,ake->he",
        weight_in,
        lax.all_gather(stacked, "ch", axis=1, tiled=True),
        preferred_element_type=jnp.float32,
    )


def shards(
    node_feats,
    edge_feats,
    send_rows,
    edge_src,
    edge_dst,
    w_edge_in,
    w_edge_out,
    w_node_in,
    w_node_out,
):
    share = node_feats.shape[0]
    node_count = node_feats.shape[1]
    domains = lax.axis_size("dom")
    nodes = node_feats
    edges = edge_feats
    for layer in range(LAYERS):
        packed = nodes[:, send_rows].reshape(share, domains, SLOTS)
        received = lax.all_to_all(packed, "dom", split_axis=1, concat_axis=1, tiled=True).reshape(
            share, domains * SLOTS
        )
        extended = jnp.concatenate([nodes, received], axis=1)
        stacked = jnp.stack([edges, extended[:, edge_src], nodes[:, edge_dst]])
        hidden = jax.nn.silu(edge_hidden(stacked, w_edge_in[layer])).astype(jnp.bfloat16)
        edges = finish(hidden, w_edge_out[layer], edges)
        gathered = (
            jnp.zeros((share, node_count), jnp.float32)
            .at[:, edge_dst]
            .add(edges.astype(jnp.float32))
        )
        both = jnp.stack([nodes, gathered.astype(jnp.bfloat16)])
        node_weight = w_node_in[layer]
        hidden_n = jnp.einsum(
            "akh,akn->hn",
            node_weight,
            lax.all_gather(both, "ch", axis=1, tiled=True),
            preferred_element_type=jnp.float32,
        )
        hidden_n = jax.nn.silu(hidden_n).astype(jnp.bfloat16)
        nodes = finish(hidden_n, w_node_out[layer], nodes)
    return (nodes, edges)


def solution(mesh):
    in_specs = (
        P("ch", "dom"),
        P("ch", "dom"),
        P("dom"),
        P("dom"),
        P("dom"),
        P(None, None, None, "ch"),
        P(None, "ch", None),
        P(None, None, None, "ch"),
        P(None, "ch", None),
    )
    out_specs = (P("ch", "dom"), P("ch", "dom"))
    return jax.shard_map(shards, mesh=mesh, in_specs=in_specs, out_specs=out_specs, check_vma=False)
```

profile of v0, /device:TPU:1, one launch (start us, length us, event | category | flops | bytes accessed | tf_op | source)
XLA Modules:
  0.0 486.4 jit_solution(14797563048734557695)
XLA Ops:
  8.9 3.2 gather_fusion
  13.0 9.2 %all-to-all-start = ((bf16[32,2,1024]{2,1,0:T(2,128)(2,1)}), bf16[32,2,1024]{2,1,0:T(2,128)(2,1)S(1)}, u32[]{:S(2)}, u32[]{:S(2)}) async-start(bf16[32,2,1024]{2,1,0:T(2,128)(2,1)} %reshape.116), calls=%async_computation | async-start | bytes 262144 | tf_op jit(solution)/shard_map/all_to_all | solution.py:54
  22.3 3.2 gather_fusion.2
  25.7 4.0 all-to-all-done
  30.1 3.2 gather_fusion.1
  34.3 44.7 %all-gather.5.cloned.1.call-done = bf16[3,512,1024]{2,1,0:T(8,128)(2,1)} async-done(((bf16[3,64,1024]{2,1,0:T(8,128)(2,1)}), bf16[3,512,1024]{2,1,0:T(8,128)(2,1)}) %all-gather.5.cloned.1.call-update) | async-done | bytes 3145744 | tf_op jit(solution)/shard_map/all_gather | solution.py:31
  84.1 39.7 %reduce-scatter.13.cloned.1.call-done = f32[64,1024]{1,0:T(8,128)} async-done(((f32[512,1024]{1,0:T(8,128)}), f32[64,1024]{1,0:T(8,128)}) %reduce-scatter.13.cloned.1.call-update) | async-done | bytes 262160
  126.2 15.7 %all-reduce.3 = (f32[1024]{0:T(1024)S(1)}, f32[1024]{0:T(1024)S(1)}) all-reduce(f32[1024]{0:T(1024)S(1)} %multiply_reduce_fusion.1, f32[1024]{0:T(1024)S(1)} %reduce_sum.72), channel_id=1, replica_groups=mesh['dom'=32,'ch'=8] {'ch'}, use_global_device_ids=true, to_apply=%region_4.5 | all-reduce | flops 2048 | bytes 16384 | tf_op jit(solution)/shard_map/psum | solution.py:20
  142.3 6.2 %scatter_custom_fusion = f32[64,768]{0,1:T(8,128)S(1)} fusion(s32[1024]{0:T(1024)S(1)} %get-tuple-element.23, bf16[64,1024]{0,1:T(8,128)(2,1)S(1)} %add_convert_fusion, f32[]{:T(128)} %constant.23.clone.1), kind=kCustom, calls=%fused_computation.21 | custom fusion | flops 131072 | bytes 458756 | tf_op jit(solution)/shard_map/scatter-add | solution.py:64
  149.3 35.5 %all-gather.7.cloned.1.call-done = bf16[2,512,768]{2,1,0:T(8,128)(2,1)} async-done(((bf16[2,64,768]{2,1,0:T(8,128)(2,1)}), bf16[2,512,768]{2,1,0:T(8,128)(2,1)}) %all-gather.7.cloned.1.call-update) | async-done | bytes 1572880 | tf_op jit(solution)/shard_map/all_gather | solution.py:71
  188.8 38.0 %reduce-scatter.15.cloned.1.call-done = f32[64,768]{1,0:T(8,128)} async-done(((f32[512,768]{1,0:T(8,128)}), f32[64,768]{1,0:T(8,128)}) %reduce-scatter.15.cloned.1.call-update) | async-done | bytes 196624
  229.0 15.1 %all-reduce.2 = (f32[768]{0:T(1024)S(1)}, f32[768]{0:T(1024)S(1)}) all-reduce(f32[768]{0:T(1024)S(1)} %multiply_reduce_fusion.3, f32[768]{0:T(1024)S(1)} %reduce_sum.74), channel_id=1, replica_groups=mesh['dom'=32,'ch'=8] {'ch'}, use_global_device_ids=true, to_apply=%region_10.11 | all-reduce | flops 1536 | bytes 12288 | tf_op jit(solution)/shard_map/psum | solution.py:20
  244.4 3.2 gather_fusion.3
  248.5 7.9 %all-to-all-start.1 = ((bf16[32,2,1024]{2,1,0:T(2,128)(2,1)}), bf16[32,2,1024]{2,1,0:T(2,128)(2,1)S(1)}, u32[]{:S(2)}, u32[]{:S(2)}) async-start(bf16[32,2,1024]{2,1,0:T(2,128)(2,1)} %reshape.118), calls=%async_computation.1 | async-start | bytes 262144 | tf_op jit(solution)/shard_map/all_to_all | solution.py:54
  256.4 3.2 gather_fusion.5
  259.6 4.1 all-to-all-done.1
  264.1 3.2 gather_fusion.4
  268.6 44.4 %all-gather.9.cloned.1.call-done = bf16[3,512,1024]{2,1,0:T(8,128)(2,1)} async-done(((bf16[3,64,1024]{2,1,0:T(8,128)(2,1)}), bf16[3,512,1024]{2,1,0:T(8,128)(2,1)}) %all-gather.9.cloned.1.call-update) | async-done | bytes 3145744 | tf_op jit(solution)/shard_map/all_gather | solution.py:31
  317.9 39.7 %reduce-scatter.17.cloned.1.call-done = f32[64,1024]{1,0:T(8,128)} async-done(((f32[512,1024]{1,0:T(8,128)}), f32[64,1024]{1,0:T(8,128)}) %reduce-scatter.17.cloned.1.call-update) | async-done | bytes 262160
  359.9 15.8 %all-reduce.1 = (f32[1024]{0:T(1024)S(1)}, f32[1024]{0:T(1024)S(1)}) all-reduce(f32[1024]{0:T(1024)S(1)} %multiply_reduce_fusion, f32[1024]{0:T(1024)S(1)} %reduce_sum.76), channel_id=1, replica_groups=mesh['dom'=32,'ch'=8] {'ch'}, use_global_device_ids=true, to_apply=%region_15.16 | all-reduce | flops 2048 | bytes 16384 | tf_op jit(solution)/shard_map/psum | solution.py:20
  376.1 6.2 %scatter_custom_fusion.1 = f32[64,768]{0,1:T(8,128)S(1)} fusion(s32[1024]{0:T(1024)S(1)} %get-tuple-element.23, bf16[64,1024]{0,1:T(8,128)(2,1)S(1)} %fusion.6, f32[]{:T(128)} %constant.23.clone.1), kind=kCustom, calls=%fused_computation.23 | custom fusion | flops 131072 | bytes 458756 | tf_op jit(solution)/shard_map/scatter-add | solution.py:64
  383.3 36.0 %all-gather.11.cloned.1.call-done = bf16[2,512,768]{2,0,1:T(2,128)(2,1)} async-done(((bf16[2,64,768]{2,0,1:T(2,128)(2,1)}), bf16[2,512,768]{2,0,1:T(2,128)(2,1)}) %all-gather.11.cloned.1.call-update) | async-done | bytes 1572880 | tf_op jit(solution)/shard_map/all_gather | solution.py:71
  424.0 37.2 %reduce-scatter.19.cloned.1.call-done = f32[64,768]{1,0:T(8,128)} async-done(((f32[512,768]{1,0:T(8,128)}), f32[64,768]{1,0:T(8,128)}) %reduce-scatter.19.cloned.1.call-update) | async-done | bytes 196624
  463.5 15.0 %all-reduce = (f32[768]{0:T(1024)S(1)}, f32[768]{0:T(1024)S(1)}) all-reduce(f32[768]{0:T(1024)S(1)} %multiply_reduce_fusion.2, f32[768]{0:T(1024)S(1)} %reduce_sum.78), channel_id=1, replica_groups=mesh['dom'=32,'ch'=8] {'ch'}, use_global_device_ids=true, to_apply=%region_21.22 | all-reduce | flops 1536 | bytes 12288 | tf_op jit(solution)/shard_map/psum | solution.py:20
  (85 shorter events, 38.0 us)
Async XLA Ops:
  7.2 15.1 %copy-start.7 = (s32[1024]{0:T(1024)S(1)}, s32[1024]{0:T(1024)}, u32[]{:S(2)}) copy-start(s32[1024]{0:T(1024)} %param.13) | copy-start | bytes 12292
  8.9 16.7 %copy-start.8 = (s32[1024]{0:T(1024)S(1)}, s32[1024]{0:T(1024)}, u32[]{:S(2)}) copy-start(s32[1024]{0:T(1024)} %param.12) | copy-start | bytes 12292
  13.0 16.7 %all-to-all-start = ((bf16[32,2,1024]{2,1,0:T(2,128)(2,1)}), bf16[32,2,1024]{2,1,0:T(2,128)(2,1)S(1)}, u32[]{:S(2)}, u32[]{:S(2)}) async-start(bf16[32,2,1024]{2,1,0:T(2,128)(2,1)} %reshape.116), calls=%async_computation | async-start | bytes 262144 | tf_op jit(solution)/shard_map/all_to_all | solution.py:54
  22.2 56.8 %all-gather.5.cloned.1.call-start = ((), (), s32[]{:S(2)}) async-start(), calls=%async_computation.6 | async-start | bytes 3538944 | tf_op jit(solution)/shard_map/all_gather | solution.py:31
  25.5 7.9 %copy-start = (bf16[64,1024]{1,0:T(8,128)(2,1)S(1)}, bf16[64,1024]{1,0:T(8,128)(2,1)}, u32[]{:S(2)}) copy-start(bf16[64,1024]{1,0:T(8,128)(2,1)} %param.10) | copy-start | bytes 393220
  30.1 49.0 %copy-start.1 = (bf16[2,3,512,64]{2,3,1,0:T(8,128)(2,1)S(1)}, bf16[2,3,512,64]{2,3,1,0:T(8,128)(2,1)}, u32[]{:S(2)}) copy-start(bf16[2,3,512,64]{2,3,1,0:T(8,128)(2,1)} %param.14) | copy-start | bytes 1179652
  30.1 49.0 %copy-start.4 = (bf16[2,64,512]{2,1,0:T(8,128)(2,1)S(1)}, bf16[2,64,512]{2,1,0:T(8,128)(2,1)}, u32[]{:S(2)}) copy-start(bf16[2,64,512]{2,1,0:T(8,128)(2,1)} %param.15) | copy-start | bytes 393220
  34.3 89.6 %reduce-scatter.13.cloned.1.call-start = ((), (), s32[]{:S(2)}) async-start(), calls=%async_computation.10 | async-start | bytes 2359296
  83.9 101.0 %all-gather.7.cloned.1.call-start = ((), (), s32[]{:S(2)}) async-start(), calls=%async_computation.7 | async-start | bytes 1769472 | tf_op jit(solution)/shard_map/all_gather | solution.py:71
  125.0 23.6 %copy-start.2 = (bf16[64,768]{1,0:T(8,128)(2,1)S(1)}, bf16[64,768]{1,0:T(8,128)(2,1)}, u32[]{:S(2)}) copy-start(bf16[64,768]{1,0:T(8,128)(2,1)} %param.9) | copy-start | bytes 294916
  125.2 59.7 %copy-start.3 = (bf16[2,2,512,64]{2,3,1,0:T(8,128)(2,1)S(1)}, bf16[2,2,512,64]{2,3,1,0:T(8,128)(2,1)}, u32[]{:S(2)}) copy-start(bf16[2,2,512,64]{2,3,1,0:T(8,128)(2,1)} %param.16) | copy-start | bytes 786436
  125.2 59.7 %copy-start.5 = (bf16[2,64,512]{2,1,0:T(8,128)(2,1)S(1)}, bf16[2,64,512]{2,1,0:T(8,128)(2,1)}, u32[]{:S(2)}) copy-start(bf16[2,64,512]{2,1,0:T(8,128)(2,1)} %param.17) | copy-start | bytes 393220
  149.3 77.5 %reduce-scatter.15.cloned.1.call-start = ((), (), s32[]{:S(2)}) async-start(), calls=%async_computation.11 | async-start | bytes 1769472
  248.5 15.3 %all-to-all-start.1 = ((bf16[32,2,1024]{2,1,0:T(2,128)(2,1)}), bf16[32,2,1024]{2,1,0:T(2,128)(2,1)S(1)}, u32[]{:S(2)}, u32[]{:S(2)}) async-start(bf16[32,2,1024]{2,1,0:T(2,128)(2,1)} %reshape.118), calls=%async_computation.1 | async-start | bytes 262144 | tf_op jit(solution)/shard_map/all_to_all | solution.py:54
  256.4 56.6 %all-gather.9.cloned.1.call-start = ((), (), s32[]{:S(2)}) async-start(), calls=%async_computation.8 | async-start | bytes 3538944 | tf_op jit(solution)/shard_map/all_gather | solution.py:31
  268.5 89.0 %reduce-scatter.17.cloned.1.call-start = ((), (), s32[]{:S(2)}) async-start(), calls=%async_computation.12 | async-start | bytes 2359296
  317.8 101.5 %all-gather.11.cloned.1.call-start = ((), (), s32[]{:S(2)}) async-start(), calls=%async_computation.9 | async-start | bytes 1769472 | tf_op jit(solution)/shard_map/all_gather | solution.py:71
  376.1 43.3 %copy-start.6 = (bf16[2,64,512]{2,1,0:T(8,128)(2,1)S(1)}, bf16[2,64,512]{2,1,0:T(8,128)(2,1)}, u32[]{:S(2)}) copy-start(bf16[2,64,512]{2,1,0:T(8,128)(2,1)} %param.17) | copy-start | bytes 393220
  383.3 78.0 %reduce-scatter.19.cloned.1.call-start = ((), (), s32[]{:S(2)}) async-start(), calls=%async_computation.13 | async-start | bytes 1769472
Sparse Core Ops, SparseCore 0:
  34.4 44.6 all-gather.4
  84.0 39.7 reduce-scatter.12
  149.4 35.4 all-gather.6
  188.9 37.8 reduce-scatter.14
  268.6 44.3 all-gather.8
  318.0 39.5 reduce-scatter.16
  383.4 35.9 all-gather.10
  423.3 37.8 reduce-scatter.18
where the time goes:
time: 488 us; the launch traced here: 486 us
  waiting for transfers between devices  324 us (66%)
  blocking collectives  61.6 us (13%)
  local copies, waits for them, and re-layouts  37.9 us (8%)
  other arithmetic  20.9 us (4%)
  starting transfers between devices  17.5 us (4%)
  between operations  14.6 us (3%)
  matrix products  10.2 us (2%)
    unnamed x12, waiting for transfers between devices  155 us
    all_gather x2, waiting for transfers between devices, edge_hidden(): lax.all_gather(stacked, 'ch', axis=1, tiled=True)  89.2 us
    all_gather x2, waiting for transfers between devices, shards(): lax.all_gather(both, 'ch', axis=1, tiled=True)  71.6 us
    psum x4, blocking collectives, finish(): lax.psum((jnp.sum(summed, axis=0), jnp.sum(summed * summed, axis=0)), 'ch')  61.6 us
    all_to_all x2, starting transfers between devices, shards(): lax.all_to_all(packed, 'dom', split_axis=1, concat_axis=1, tiled=True)  17.1 us
    unnamed x34, local copies, waits for them, and re-layouts  16.5 us
    gather x6, local copies, waits for them, and re-layouts, shards(): stacked = jnp.stack([edges, extended[:, edge_src], nodes[:, edge_dst]])  13.1 us
    scatter-add x2, other arithmetic, shards(): gathered = jnp.zeros((share, node_count), jnp.float32).at[:, edge_dst].ad...  12.3 us
  transfers between devices with their start and end apart: 10, of which 10 were waited for; matrix products, arithmetic and copies ran while one was open for 2% of the time, Pallas kernels for 0%

commit v1 on v0

v1 whole, which is shorter than its diff:
```python
import jax
import jax.numpy as jnp
from jax import lax
from jax.sharding import PartitionSpec as P

LATENT = 512
SLOTS = 32
LAYERS = 2
BF = jnp.bfloat16
F32 = jnp.float32

CORE = [(c, c ^ 1) for c in range(8)]
Z_GROUPS = [[k, 2 + k, 4 + k, 6 + k] for k in (0, 1)]
XY_GROUPS = [[16 * z + i for i in range(16)] for z in (0, 1)]


def z_shift(s):
    return [(c, ((c // 2 + s) % 4) * 2 + c % 2) for c in range(8)]


def swap(x):
    return lax.ppermute(x, "ch", CORE)


def z_gather(x, zi):
    prev = lax.ppermute(x, "ch", z_shift(1))
    nxt = lax.ppermute(x, "ch", z_shift(3))
    far_a = lax.ppermute(prev[:32], "ch", z_shift(1))
    far_b = lax.ppermute(nxt[32:], "ch", z_shift(3))
    far = jnp.concatenate([far_a, far_b])
    rel = jnp.stack([x, nxt, far, prev])
    return lax.dynamic_slice_in_dim(jnp.concatenate([rel, rel]), (4 - zi) % 4, 4, 0)


def interleave(own, other, k):
    even = jnp.where(k == 0, own, other)
    odd = jnp.where(k == 0, other, own)
    return jnp.stack([even, odd], axis=1).reshape(LATENT, own.shape[-1])


def dot(a, b, ca, cb):
    return lax.dot_general(a, b, (((ca,), (cb,)), ((), ())), preferred_element_type=F32)


def norm_add(msg, residual):
    mean = jnp.mean(msg, axis=0, keepdims=True)
    var = jnp.mean(msg * msg, axis=0, keepdims=True) - mean * mean
    return (residual.astype(F32) + (msg - mean) * lax.rsqrt(var + 1e-05)).astype(BF)


def one_hot(idx, n):
    return (lax.broadcasted_iota(jnp.int32, (n, idx.shape[0]), 0) == idx[None, :]).astype(BF)


def weight_rows(w_in, w_out):
    blocks = w_in.shape[0]
    return [w_in[b].T for b in range(blocks)] + [w_out]


def shards(node_feats, edge_feats, send_rows, edge_src, edge_dst, w_edge_in, w_edge_out, w_node_in, w_node_out):
    d = lax.axis_index("dom")
    c = lax.axis_index("ch")
    j = d % 16
    zi = c // 2
    k = c % 2
    n_nodes = node_feats.shape[1]
    n_edges = edge_feats.shape[1]

    v_half = z_gather(node_feats, zi)
    v_own = v_half.reshape(256, n_nodes)
    a_rows = [jnp.concatenate(weight_rows(w_edge_in[layer], w_edge_out[layer])) for layer in range(LAYERS)]
    a_mine = [lax.dynamic_slice_in_dim(r, j * 16, 16, 0) for r in a_rows]
    n_mats = jnp.stack([jnp.stack(weight_rows(w_node_in[layer], w_node_out[layer])) for layer in range(LAYERS)])
    n_mine = lax.dynamic_slice(n_mats, (j // 8, 0, (j % 8) * 8, 0), (1, 3, 8, LATENT)).reshape(24, LATENT)
    mine = jnp.concatenate(a_mine + [n_mine])
    mine = lax.all_to_all(jnp.broadcast_to(mine[None], (4,) + mine.shape), "ch", 0, 0, axis_index_groups=Z_GROUPS, tiled=True)

    def spread(x):
        return lax.all_to_all(
            jnp.broadcast_to(x[None], (16,) + x.shape), "dom", 0, 0, axis_index_groups=XY_GROUPS, tiled=True
        )

    edge_w = []
    for layer in range(LAYERS):
        edge_w.append(spread(mine[:, layer * 16 : layer * 16 + 16]).reshape(4, 256, LATENT))
    node_all = spread(mine[:, 32:56]).reshape(2, 8, 4, 3, 8, LATENT)
    node_w = [[node_all[layer, :, :, m].reshape(256, LATENT) for m in range(3)] for layer in range(LAYERS)]

    oh_send = one_hot(send_rows, n_nodes)
    oh_src = one_hot(edge_src, n_nodes + n_edges)
    oh_dst = one_hot(edge_dst, n_nodes)

    def halo(x):
        rows = dot(oh_send, x, 0, 1).astype(BF)
        return lax.all_to_all(rows, "dom", 0, 0, tiled=True)

    halo_own = halo(v_own)
    v_other = swap(v_half)
    e_half = z_gather(edge_feats, zi)
    e_other = swap(e_half)
    halo_other = swap(halo_own)
    nodes = interleave(v_half, v_other, k)
    edges = interleave(e_half, e_other, k)
    halo_t = interleave(
        halo_own.T.reshape(4, 64, -1), halo_other.T.reshape(4, 64, -1), k
    )

    for layer in range(LAYERS):
        w_e, w_s, w_r, w_o = (edge_w[layer][m] for m in range(4))
        sender = dot(w_s, nodes, 1, 0).astype(BF)
        if layer == 0:
            far = dot(w_s, halo_t, 1, 0).astype(BF)
            far_part = dot(far, oh_src[n_nodes:], 1, 0)
        else:
            far_part = dot(halo(sender), oh_src[n_nodes:], 0, 0)
        receiver = dot(w_r, nodes, 1, 0).astype(BF)
        pre = dot(w_e, edges, 1, 0) + dot(sender, oh_src[:n_nodes], 1, 0) + far_part + dot(receiver, oh_dst, 1, 0)
        hidden = jax.nn.silu(pre).astype(BF)
        msg = dot(w_o, hidden, 0, 0) + dot(swap(w_o), swap(hidden), 0, 0)
        edges = norm_add(msg, edges)
        agg = dot(edges, oh_dst, 1, 1).astype(BF)
        n_v, n_a, n_o = node_w[layer]
        hidden_n = jax.nn.silu(dot(n_v, nodes, 1, 0) + dot(n_a, agg, 1, 0)).astype(BF)
        msg_n = dot(n_o, hidden_n, 0, 0) + dot(swap(n_o), swap(hidden_n), 0, 0)
        nodes = norm_add(msg_n, nodes)
    return (
        lax.dynamic_slice_in_dim(nodes, c * 64, 64, 0),
        lax.dynamic_slice_in_dim(edges, c * 64, 64, 0),
    )


def solution(mesh):
    in_specs = (
        P("ch", "dom"),
        P("ch", "dom"),
        P("dom"),
        P("dom"),
        P("dom"),
        P(None, None, None, "ch"),
        P(None, "ch", None),
        P(None, None, None, "ch"),
        P(None, "ch", None),
    )
    out_specs = (P("ch", "dom"), P("ch", "dom"))
    return jax.shard_map(shards, mesh=mesh, in_specs=in_specs, out_specs=out_specs, check_vma=False)
```

time: 488 us -> 172 us (0.35)
  waiting for transfers between devices: 324 us -> 29.4 us
  blocking collectives: 61.6 us -> 0 us
  starting transfers between devices: 17.5 us -> 69.9 us
  matrix products: 10.2 us -> 40.6 us
  local copies, waits for them, and re-layouts: 37.9 us -> 20.3 us
  between operations: 14.6 us -> 1.39 us
  other arithmetic: 20.9 us -> 8.79 us
    all_gather x4 -> x0, waiting for transfers between devices: 161 us -> none  [the longest x2 89.2 us: edge_hidden(): lax.all_gather(stacked, 'ch', axis=1, tiled=True)]
    unnamed x12 -> x0, waiting for transfers between devices: 155 us -> none
    psum x4 -> x0, blocking collectives: 61.6 us -> none  [finish(): lax.psum((jnp.sum(summed, axis=0), jnp.sum(summed * summed, axis=0)), 'ch')]
    ppermute x0 -> x19, starting transfers between devices: none -> 34.3 us  [the longest x11 16.2 us: swap(): return lax.ppermute(x, 'ch', CORE)]
    dot_general x4 -> x23, matrix products: 10.2 us -> 40.6 us  [dot(): lax.dot_general(a, b, (((ca,), (cb,)), ((), ())), preferred_element_type=...]
    gather x8 -> x0, local copies, waits for them, and re-layouts: 19.5 us -> none  [the longest x6 13.1 us: shards(): stacked = jnp.stack([edges, extended[:, edge_src], nodes[:, edge_dst]])]
    all_to_all x2 -> x6, waiting for transfers between devices: 8.14 us -> 26.7 us  [the longest x2 15.5 us: halo(): return lax.all_to_all(rows, 'dom', 0, 0, tiled=True)]
    all_to_all x2 -> x6, starting transfers between devices: 17.1 us -> 35.6 us  [the longest x3 15.6 us: spread(): lax.all_to_all(jnp.broadcast_to(x[None], (16,) + x.shape), 'dom', 0, 0, a...]
  transfers between devices with their start and end apart: 10 -> 25, of which waited for: 10 -> 6; matrix products, arithmetic and copies ran while one was open for 2% -> 37% of each run, Pallas kernels for 0% -> 0%
where the time goes in v1:
time: 172 us; the launch traced here: 170 us
  starting transfers between devices  69.9 us (41%)
  matrix products  40.6 us (24%)
  waiting for transfers between devices  29.4 us (17%)
  local copies, waits for them, and re-layouts  20.3 us (12%)
  other arithmetic  8.79 us (5%)
    dot_general x23, matrix products, dot(): lax.dot_general(a, b, (((ca,), (cb,)), ((), ())), preferred_element_type=...  40.6 us
    ppermute x11, starting transfers between devices, swap(): return lax.ppermute(x, 'ch', CORE)  16.2 us
    all_to_all x3, starting transfers between devices, spread(): lax.all_to_all(jnp.broadcast_to(x[None], (16,) + x.shape), 'dom', 0, 0, a...  15.6 us
    all_to_all x2, waiting for transfers between devices, halo(): return lax.all_to_all(rows, 'dom', 0, 0, tiled=True)  15.5 us
    all_to_all x2, starting transfers between devices, halo(): return lax.all_to_all(rows, 'dom', 0, 0, tiled=True)  14.3 us
    all_to_all x3, waiting for transfers between devices, spread(): lax.all_to_all(jnp.broadcast_to(x[None], (16,) + x.shape), 'dom', 0, 0, a...  11.2 us
    all_to_all x1, starting transfers between devices, shards(): lax.all_to_all(jnp.broadcast_to(mine[None], (4,) + mine.shape), 'ch', 0,...  5.64 us
    ppermute x2, starting transfers between devices, z_gather(): nxt = lax.ppermute(x, 'ch', z_shift(3))  5.61 us
  transfers between devices with their start and end apart: 25, of which 6 were waited for; matrix products, arithmetic and copies ran while one was open for 37% of the time, Pallas kernels for 0%

profile of v1, /device:TPU:1, one launch (start us, length us, event | category | flops | bytes accessed | tf_op | source)
XLA Modules:
  0.0 170.4 jit_solution(12468451011751761144)
XLA Ops:
  0.6 3.9 %collective-permute-start.6 = (bf16[64,1024]{1,0:T(8,128)(2,1)}, bf16[64,1024]{1,0:T(8,128)(2,1)S(1)}, u32[]{:S(2)}, u32[]{:S(2)}) collective-permute-start(bf16[64,1024]{1,0:T(8,128)(2,1)} %param.10), channel_id=1, source_target_pairs={{0,2},{1,3},{2,4},{3,5},{4,6},{5,7},{6,0},{7,1},{8,10},{9,11},{10,... | collective-permute-start | bytes 393224 | tf_op jit(solution)/shard_map/ppermute | solution.py:26
  4.5 3.1 %collective-permute-start.5 = (bf16[64,1024]{1,0:T(8,128)(2,1)}, bf16[64,1024]{1,0:T(8,128)(2,1)S(1)}, u32[]{:S(2)}, u32[]{:S(2)}) collective-permute-start(bf16[64,1024]{1,0:T(8,128)(2,1)} %param.10), channel_id=1, source_target_pairs={{0,6},{1,7},{2,0},{3,1},{4,2},{5,3},{6,4},{7,5},{8,14},{9,15},{10,... | collective-permute-start | bytes 393224 | tf_op jit(solution)/shard_map/ppermute | solution.py:27
  8.7 2.5 %collective-permute-start = (bf16[64,768]{1,0:T(8,128)(2,1)}, bf16[64,768]{1,0:T(8,128)(2,1)S(1)}, u32[]{:S(2)}, u32[]{:S(2)}) collective-permute-start(bf16[64,768]{1,0:T(8,128)(2,1)} %param.9), channel_id=1, source_target_pairs={{0,6},{1,7},{2,0},{3,1},{4,2},{5,3},{6,4},{7,5},{8,14},{9,15},{10,... | collective-permute-start | bytes 294920 | tf_op jit(solution)/shard_map/ppermute | solution.py:27
  16.0 5.6 %all-to-all-start = ((bf16[4,56,512]{2,1,0:T(8,128)(2,1)}), bf16[4,56,512]{2,1,0:T(8,128)(2,1)S(1)}, u32[]{:S(2)}, u32[]{:S(2)}) async-start(bf16[4,56,512]{2,1,0:T(8,128)(2,1)} %broadcast_in_dim.8), calls=%async_computation | async-start | bytes 458752 | tf_op jit(solution)/shard_map/all_to_all | solution.py:76
  21.8 2.4 %collective-permute-start.2 = (bf16[32,768]{1,0:T(8,128)(2,1)S(1)}, bf16[32,768]{1,0:T(8,128)(2,1)S(1)}, u32[]{:S(2)}, u32[]{:S(2)}) collective-permute-start(bf16[32,768]{1,0:T(8,128)(2,1)S(1)} %slice.182), channel_id=1, source_target_pairs={{0,2},{1,3},{2,4},{3,5},{4,6},{5,7},{6,0},{7,1},{8,10},{9,11},{10,... | collective-permute-start | bytes 147464 | tf_op jit(solution)/shard_map/ppermute | solution.py:28
  32.2 2.9 %collective-permute-start.4 = (bf16[4,64,768]{2,1,0:T(8,128)(2,1)}, bf16[4,64,768]{2,1,0:T(8,128)(2,1)}, u32[]{:S(2)}, u32[]{:S(2)}) collective-permute-start(bf16[4,64,768]{2,1,0:T(8,128)(2,1)} %constant_dynamic-slice_fusion.2), channel_id=1, source_target_pairs={{0,1},{1,0},{2,3},{3,2},{4,5},{5,4},{6,7},{7,6},{8,9},{9,8},{10,11... | collective-permute-start | bytes 1179656 | tf_op jit(solution)/shard_map/ppermute | solution.py:22
  37.6 9.5 %all-to-all-start.3 = ((bf16[32,32,256]{2,1,0:T(8,128)(2,1)}), bf16[32,32,256]{2,1,0:T(8,128)(2,1)S(1)}, u32[]{:S(2)}, u32[]{:S(2)}) async-start(bf16[32,32,256]{2,1,0:T(8,128)(2,1)} %bitcast.51), calls=%async_computation.3 | async-start | bytes 1048576 | tf_op jit(solution)/shard_map/all_to_all | solution.py:95
  49.0 8.6 %all-to-all-done.3 = bf16[32,32,256]{2,1,0:T(8,128)(2,1)S(1)} async-done(((bf16[32,32,256]{2,1,0:T(8,128)(2,1)}), bf16[32,32,256]{2,1,0:T(8,128)(2,1)S(1)}, u32[]{:S(2)}, u32[]{:S(2)}) %all-to-all-start.3) | async-done | bytes 524320 | tf_op jit(solution)/shard_map/all_to_all | solution.py:95
  58.7 3.7 %all-to-all-start.2 = ((bf16[16,4,16,512]{3,2,1,0:T(8,128)(2,1)}), bf16[16,4,16,512]{3,2,1,0:T(8,128)(2,1)S(1)}, u32[]{:S(2)}, u32[]{:S(2)}) async-start(bf16[16,4,16,512]{3,2,1,0:T(8,128)(2,1)} %broadcast_in_dim.10), calls=%async_computation.2 | async-start | bytes 2097152 | tf_op jit(solution)/shard_map/all_to_all | solution.py:79
  62.4 2.8 %iota_compare_fusion = pred[1792,1024]{1,0:T(32,128)(4,1)} fusion(s32[1024]{0:T(1024)S(1)} %copy-done.17), kind=kLoop, calls=%fused_computation | loop fusion | flops 1835008 | bytes 1839104 | tf_op jit(solution)/shard_map/eq | solution.py:52
  70.4 7.1 %all-to-all-done.2 = bf16[16,4,16,512]{3,2,1,0:T(8,128)(2,1)S(1)} async-done(((bf16[16,4,16,512]{3,2,1,0:T(8,128)(2,1)}), bf16[16,4,16,512]{3,2,1,0:T(8,128)(2,1)S(1)}, u32[]{:S(2)}, u32[]{:S(2)}) %all-to-all-start.2) | async-done | bytes 1048608 | tf_op jit(solution)/shard_map/all_to_all | solution.py:79
  78.8 5.0 %all-to-all-start.1 = ((bf16[16,4,24,512]{3,2,1,0:T(8,128)(2,1)}), bf16[16,4,24,512]{3,2,1,0:T(8,128)(2,1)}, u32[]{:S(2)}, u32[]{:S(2)}) async-start(bf16[16,4,24,512]{3,2,1,0:T(8,128)(2,1)} %broadcast_in_dim.9), calls=%async_computation.1 | async-start | bytes 3145728 | tf_op jit(solution)/shard_map/all_to_all | solution.py:79
  84.9 2.9 %collective-permute-start.11 = (bf16[256,512]{1,0:T(8,128)(2,1)}, bf16[256,512]{1,0:T(8,128)(2,1)}, u32[]{:S(2)}, u32[]{:S(2)}) collective-permute-start(bf16[256,512]{1,0:T(8,128)(2,1)} %bitcast.47), channel_id=1, source_target_pairs={{0,1},{1,0},{2,3},{3,2},{4,5},{5,4},{6,7},{7,6},{8,9},{9,8},{10,11... | collective-permute-start | bytes 786440 | tf_op jit(solution)/shard_map/ppermute | solution.py:22
  87.8 2.9 %fusion.7 = f32[256,1024]{1,0:T(8,128)} fusion(s32[1024]{0:T(1024)S(1)} %copy-done.19, bf16[256,512]{1,0:T(8,128)(2,1)} %bitcast.193, bf16[512,768]{1,0:T(8,128)(2,1)S(1)} %bitcast.172), kind=kOutput, calls=%fused_computation.9 | convolution fusion | flops 604962816 | bytes 2101248 | tf_op jit(solution)/shard_map/dot_general | solution.py:42
  94.9 3.6 %fusion.2 = f32[256,1024]{1,0:T(8,128)} fusion(pred[1792,1024]{1,0:T(32,128)(4,1)} %iota_compare_fusion, bf16[256,512]{1,0:T(8,128)(2,1)S(1)} %bitcast.191, bf16[512,1024]{1,0:T(8,128)(2,1)} %bitcast.184), kind=kOutput, calls=%fused_computation.3 | convolution fusion | flops 805568512 | bytes 3407872 | tf_op jit(solution)/shard_map/dot_general | solution.py:42
  98.5 3.7 %multiply_convert_fusion.1 = bf16[256,1024]{1,0:T(8,128)(2,1)} fusion(f32[256,1024]{1,0:T(8,128)} %fusion.7, f32[256,1024]{1,0:T(8,128)} %fusion.2, f32[256,1024]{1,0:T(8,128)S(1)} %copy-done.5, pred[1792,1024]{1,0:T(32,128)(4,1)} %iota_compare_fusion, bf16[256,512]{1,0:T(8,128)(2,1)S(1)} %bitcast.192, bf16[512,768]{1,0:T(8,128)(2,1)S(1)} %bitcast.173), kind=kOutput, calls=%fused_computation.55 | convolution fusion | flops 606273536 | bytes 5505024 | tf_op jit(solution)/shard_map/dot_general | solution.py:42
  105.0 6.9 %all-to-all-start.4 = ((bf16[16,4,16,512]{3,2,1,0:T(8,128)(2,1)}), bf16[16,4,16,512]{3,2,1,0:T(8,128)(2,1)}, u32[]{:S(2)}, u32[]{:S(2)}) async-start(bf16[16,4,16,512]{3,2,1,0:T(8,128)(2,1)} %broadcast_in_dim.11), calls=%async_computation.4 | async-start | bytes 2097152 | tf_op jit(solution)/shard_map/all_to_all | solution.py:79
  111.9 2.5 %fusion.72 = (bf16[1,8,4,1,8,512]{5,4,3,2,1,0:T(8,128)(2,1)}, bf16[1,8,4,1,8,512]{5,4,3,2,1,0:T(8,128)(2,1)}, bf16[1,8,4,1,8,512]{5,4,3,2,1,0:T(8,128)(2,1)S(1)}...) fusion(bf16[2,8,4,3,8,512]{5,4,3,2,1,0:T(8,128)(2,1)} %bitcast.36), kind=kLoop, calls=%fused_computation.135 | loop fusion | bytes 3145728 | tf_op jit(solution)/shard_map/slice | solution.py:87
  122.8 4.1 %all-to-all-done.4 = bf16[16,4,16,512]{3,2,1,0:T(8,128)(2,1)} async-done(((bf16[16,4,16,512]{3,2,1,0:T(8,128)(2,1)}), bf16[16,4,16,512]{3,2,1,0:T(8,128)(2,1)}, u32[]{:S(2)}, u32[]{:S(2)}) %all-to-all-start.4) | async-done | bytes 1048608 | tf_op jit(solution)/shard_map/all_to_all | solution.py:79
  129.0 3.4 %collective-permute-start.13 = (bf16[256,512]{1,0:T(8,128)(2,1)S(1)}, bf16[256,512]{1,0:T(8,128)(2,1)S(1)}, u32[]{:S(2)}, u32[]{:S(2)}) collective-permute-start(bf16[256,512]{1,0:T(8,128)(2,1)S(1)} %bitcast.181), channel_id=1, source_target_pairs={{0,1},{1,0},{2,3},{3,2},{4,5},{5,4},{6,7},{7,6},{8,9},{9,8},{10,11... | collective-permute-start | bytes 786440 | tf_op jit(solution)/shard_map/ppermute | solution.py:22
  137.1 4.8 %all-to-all-start.5 = ((bf16[32,32,256]{2,1,0:T(8,128)(2,1)}), bf16[32,32,256]{2,1,0:T(8,128)(2,1)}, u32[]{:S(2)}, u32[]{:S(2)}) async-start(bf16[32,32,256]{2,1,0:T(8,128)(2,1)} %bitcast.65), calls=%async_computation.5 | async-start | bytes 1048576 | tf_op jit(solution)/shard_map/all_to_all | solution.py:95
  143.0 2.9 %fusion.5 = f32[256,1024]{1,0:T(8,128)} fusion(s32[1024]{0:T(1024)S(1)} %copy-done.19, bf16[256,512]{1,0:T(8,128)(2,1)} %bitcast.190, bf16[512,768]{1,0:T(8,128)(2,1)S(1)} %add_convert_fusion.2), kind=kOutput, calls=%fused_computation.7 | convolution fusion | flops 604962816 | bytes 2101248 | tf_op jit(solution)/shard_map/dot_general | solution.py:42
  145.9 6.8 %all-to-all-done.5 = bf16[32,32,256]{2,1,0:T(8,128)(2,1)} async-done(((bf16[32,32,256]{2,1,0:T(8,128)(2,1)}), bf16[32,32,256]{2,1,0:T(8,128)(2,1)}, u32[]{:S(2)}, u32[]{:S(2)}) %all-to-all-start.5) | async-done | bytes 524320 | tf_op jit(solution)/shard_map/all_to_all | solution.py:95
  163.8 2.6 %multiply_convert_fusion.2 = bf16[256,768]{1,0:T(8,128)(2,1)S(1)} fusion(f32[256,768]{1,0:T(8,128)} %fusion.81, bf16[256,512]{1,0:T(8,128)(2,1)S(1)} %bitcast.188, bf16[512,1024]{1,0:T(8,128)(2,1)S(1)} %add_convert_fusion, s32[1024]{0:T(1024)S(1)} %copy-done.19), kind=kOutput, calls=%fused_computation.57 | convolution fusion | flops 1008992256 | bytes 2494464 | tf_op jit(solution)/shard_map/dot_general | solution.py:42
  (152 shorter events, 64.5 us)
Async XLA Ops:
  0.6 24.9 %collective-permute-start.6 = (bf16[64,1024]{1,0:T(8,128)(2,1)}, bf16[64,1024]{1,0:T(8,128)(2,1)S(1)}, u32[]{:S(2)}, u32[]{:S(2)}) collective-permute-start(bf16[64,1024]{1,0:T(8,128)(2,1)} %param.10), channel_id=1, source_target_pairs={{0,2},{1,3},{2,4},{3,5},{4,6},{5,7},{6,0},{7,1},{8,10},{9,11},{10,... | collective-permute-start | bytes 393224 | tf_op jit(solution)/shard_map/ppermute | solution.py:26
  4.5 23.2 %collective-permute-start.5 = (bf16[64,1024]{1,0:T(8,128)(2,1)}, bf16[64,1024]{1,0:T(8,128)(2,1)S(1)}, u32[]{:S(2)}, u32[]{:S(2)}) collective-permute-start(bf16[64,1024]{1,0:T(8,128)(2,1)} %param.10), channel_id=1, source_target_pairs={{0,6},{1,7},{2,0},{3,1},{4,2},{5,3},{6,4},{7,5},{8,14},{9,15},{10,... | collective-permute-start | bytes 393224 | tf_op jit(solution)/shard_map/ppermute | solution.py:27
  7.6 14.1 %collective-permute-start.1 = (bf16[64,768]{1,0:T(8,128)(2,1)}, bf16[64,768]{1,0:T(8,128)(2,1)S(1)}, u32[]{:S(2)}, u32[]{:S(2)}) collective-permute-start(bf16[64,768]{1,0:T(8,128)(2,1)} %param.9), channel_id=1, source_target_pairs={{0,2},{1,3},{2,4},{3,5},{4,6},{5,7},{6,0},{7,1},{8,10},{9,11},{10,... | collective-permute-start | bytes 294920 | tf_op jit(solution)/shard_map/ppermute | solution.py:26
  8.7 15.5 %collective-permute-start = (bf16[64,768]{1,0:T(8,128)(2,1)}, bf16[64,768]{1,0:T(8,128)(2,1)S(1)}, u32[]{:S(2)}, u32[]{:S(2)}) collective-permute-start(bf16[64,768]{1,0:T(8,128)(2,1)} %param.9), channel_id=1, source_target_pairs={{0,6},{1,7},{2,0},{3,1},{4,2},{5,3},{6,4},{7,5},{8,14},{9,15},{10,... | collective-permute-start | bytes 294920 | tf_op jit(solution)/shard_map/ppermute | solution.py:27
  16.0 21.6 %all-to-all-start = ((bf16[4,56,512]{2,1,0:T(8,128)(2,1)}), bf16[4,56,512]{2,1,0:T(8,128)(2,1)S(1)}, u32[]{:S(2)}, u32[]{:S(2)}) async-start(bf16[4,56,512]{2,1,0:T(8,128)(2,1)} %broadcast_in_dim.8), calls=%async_computation | async-start | bytes 458752 | tf_op jit(solution)/shard_map/all_to_all | solution.py:76
  21.8 7.6 %collective-permute-start.2 = (bf16[32,768]{1,0:T(8,128)(2,1)S(1)}, bf16[32,768]{1,0:T(8,128)(2,1)S(1)}, u32[]{:S(2)}, u32[]{:S(2)}) collective-permute-start(bf16[32,768]{1,0:T(8,128)(2,1)S(1)} %slice.182), channel_id=1, source_target_pairs={{0,2},{1,3},{2,4},{3,5},{4,6},{5,7},{6,0},{7,1},{8,10},{9,11},{10,... | collective-permute-start | bytes 147464 | tf_op jit(solution)/shard_map/ppermute | solution.py:28
  24.2 7.1 %collective-permute-start.3 = (bf16[32,768]{1,0:T(8,128)(2,1)S(1)}, bf16[32,768]{1,0:T(8,128)(2,1)S(1)}, u32[]{:S(2)}, u32[]{:S(2)}) collective-permute-start(bf16[32,768]{1,0:T(8,128)(2,1)S(1)} %slice.183), channel_id=1, source_target_pairs={{0,6},{1,7},{2,0},{3,1},{4,2},{5,3},{6,4},{7,5},{8,14},{9,15},{10,... | collective-permute-start | bytes 147464 | tf_op jit(solution)/shard_map/ppermute | solution.py:29
  25.6 12.0 %collective-permute-start.7 = (bf16[32,1024]{1,0:T(8,128)(2,1)S(1)}, bf16[32,1024]{1,0:T(8,128)(2,1)S(1)}, u32[]{:S(2)}, u32[]{:S(2)}) collective-permute-start(bf16[32,1024]{1,0:T(8,128)(2,1)S(1)} %slice.188), channel_id=1, source_target_pairs={{0,2},{1,3},{2,4},{3,5},{4,6},{5,7},{6,0},{7,1},{8,10},{9,11},{10,... | collective-permute-start | bytes 196616 | tf_op jit(solution)/shard_map/ppermute | solution.py:28
  27.7 9.8 %collective-permute-start.8 = (bf16[32,1024]{1,0:T(8,128)(2,1)S(1)}, bf16[32,1024]{1,0:T(8,128)(2,1)S(1)}, u32[]{:S(2)}, u32[]{:S(2)}) collective-permute-start(bf16[32,1024]{1,0:T(8,128)(2,1)S(1)} %slice.189), channel_id=1, source_target_pairs={{0,6},{1,7},{2,0},{3,1},{4,2},{5,3},{6,4},{7,5},{8,14},{9,15},{10,... | collective-permute-start | bytes 196616 | tf_op jit(solution)/shard_map/ppermute | solution.py:29
  32.2 33.0 %collective-permute-start.4 = (bf16[4,64,768]{2,1,0:T(8,128)(2,1)}, bf16[4,64,768]{2,1,0:T(8,128)(2,1)}, u32[]{:S(2)}, u32[]{:S(2)}) collective-permute-start(bf16[4,64,768]{2,1,0:T(8,128)(2,1)} %constant_dynamic-slice_fusion.2), channel_id=1, source_target_pairs={{0,1},{1,0},{2,3},{3,2},{4,5},{5,4},{6,7},{7,6},{8,9},{9,8},{10,11... | collective-permute-start | bytes 1179656 | tf_op jit(solution)/shard_map/ppermute | solution.py:22
  37.6 20.0 %all-to-all-start.3 = ((bf16[32,32,256]{2,1,0:T(8,128)(2,1)}), bf16[32,32,256]{2,1,0:T(8,128)(2,1)S(1)}, u32[]{:S(2)}, u32[]{:S(2)}) async-start(bf16[32,32,256]{2,1,0:T(8,128)(2,1)} %bitcast.51), calls=%async_computation.3 | async-start | bytes 1048576 | tf_op jit(solution)/shard_map/all_to_all | solution.py:95
  48.0 18.4 %collective-permute-start.9 = (bf16[4,64,1024]{2,1,0:T(8,128)(2,1)}, bf16[4,64,1024]{2,1,0:T(8,128)(2,1)}, u32[]{:S(2)}, u32[]{:S(2)}) collective-permute-start(bf16[4,64,1024]{2,1,0:T(8,128)(2,1)} %constant_dynamic-slice_fusion.1), channel_id=1, source_target_pairs={{0,1},{1,0},{2,3},{3,2},{4,5},{5,4},{6,7},{7,6},{8,9},{9,8},{10,11... | collective-permute-start | bytes 1572872 | tf_op jit(solution)/shard_map/ppermute | solution.py:22
  58.7 18.8 %all-to-all-start.2 = ((bf16[16,4,16,512]{3,2,1,0:T(8,128)(2,1)}), bf16[16,4,16,512]{3,2,1,0:T(8,128)(2,1)S(1)}, u32[]{:S(2)}, u32[]{:S(2)}) async-start(bf16[16,4,16,512]{3,2,1,0:T(8,128)(2,1)} %broadcast_in_dim.10), calls=%async_computation.2 | async-start | bytes 2097152 | tf_op jit(solution)/shard_map/all_to_all | solution.py:79
  68.1 24.0 %collective-permute-start.10 = (bf16[1024,256]{1,0:T(8,128)(2,1)S(1)}, bf16[1024,256]{1,0:T(8,128)(2,1)}, u32[]{:S(2)}, u32[]{:S(2)}) collective-permute-start(bf16[1024,256]{1,0:T(8,128)(2,1)S(1)} %bitcast.175), channel_id=1, source_target_pairs={{0,1},{1,0},{2,3},{3,2},{4,5},{5,4},{6,7},{7,6},{8,9},{9,8},{10,11... | collective-permute-start | bytes 1572872 | tf_op jit(solution)/shard_map/ppermute | solution.py:22
  78.8 25.0 %all-to-all-start.1 = ((bf16[16,4,24,512]{3,2,1,0:T(8,128)(2,1)}), bf16[16,4,24,512]{3,2,1,0:T(8,128)(2,1)}, u32[]{:S(2)}, u32[]{:S(2)}) async-start(bf16[16,4,24,512]{3,2,1,0:T(8,128)(2,1)} %broadcast_in_dim.9), calls=%async_computation.1 | async-start | bytes 3145728 | tf_op jit(solution)/shard_map/all_to_all | solution.py:79
  84.9 30.7 %collective-permute-start.11 = (bf16[256,512]{1,0:T(8,128)(2,1)}, bf16[256,512]{1,0:T(8,128)(2,1)}, u32[]{:S(2)}, u32[]{:S(2)}) collective-permute-start(bf16[256,512]{1,0:T(8,128)(2,1)} %bitcast.47), channel_id=1, source_target_pairs={{0,1},{1,0},{2,3},{3,2},{4,5},{5,4},{6,7},{7,6},{8,9},{9,8},{10,11... | collective-permute-start | bytes 786440 | tf_op jit(solution)/shard_map/ppermute | solution.py:22
  102.2 13.4 %collective-permute-start.12 = (bf16[256,1024]{1,0:T(8,128)(2,1)}, bf16[256,1024]{1,0:T(8,128)(2,1)}, u32[]{:S(2)}, u32[]{:S(2)}) collective-permute-start(bf16[256,1024]{1,0:T(8,128)(2,1)} %multiply_convert_fusion.1), channel_id=1, source_target_pairs={{0,1},{1,0},{2,3},{3,2},{4,5},{5,4},{6,7},{7,6},{8,9},{9,8},{10,11... | collective-permute-start | bytes 1572872 | tf_op jit(solution)/shard_map/ppermute | solution.py:22
  105.0 21.9 %all-to-all-start.4 = ((bf16[16,4,16,512]{3,2,1,0:T(8,128)(2,1)}), bf16[16,4,16,512]{3,2,1,0:T(8,128)(2,1)}, u32[]{:S(2)}, u32[]{:S(2)}) async-start(bf16[16,4,16,512]{3,2,1,0:T(8,128)(2,1)} %broadcast_in_dim.11), calls=%async_computation.4 | async-start | bytes 2097152 | tf_op jit(solution)/shard_map/all_to_all | solution.py:79
  120.7 13.2 %collective-permute-start.14 = (bf16[256,768]{1,0:T(8,128)(2,1)}, bf16[256,768]{1,0:T(8,128)(2,1)S(1)}, u32[]{:S(2)}, u32[]{:S(2)}) collective-permute-start(bf16[256,768]{1,0:T(8,128)(2,1)} %multiply_convert_fusion.3), channel_id=1, source_target_pairs={{0,1},{1,0},{2,3},{3,2},{4,5},{5,4},{6,7},{7,6},{8,9},{9,8},{10,11... | collective-permute-start | bytes 1179656 | tf_op jit(solution)/shard_map/ppermute | solution.py:22
  129.0 4.8 %collective-permute-start.13 = (bf16[256,512]{1,0:T(8,128)(2,1)S(1)}, bf16[256,512]{1,0:T(8,128)(2,1)S(1)}, u32[]{:S(2)}, u32[]{:S(2)}) collective-permute-start(bf16[256,512]{1,0:T(8,128)(2,1)S(1)} %bitcast.181), channel_id=1, source_target_pairs={{0,1},{1,0},{2,3},{3,2},{4,5},{5,4},{6,7},{7,6},{8,9},{9,8},{10,11... | collective-permute-start | bytes 786440 | tf_op jit(solution)/shard_map/ppermute | solution.py:22
  137.1 15.6 %all-to-all-start.5 = ((bf16[32,32,256]{2,1,0:T(8,128)(2,1)}), bf16[32,32,256]{2,1,0:T(8,128)(2,1)}, u32[]{:S(2)}, u32[]{:S(2)}) async-start(bf16[32,32,256]{2,1,0:T(8,128)(2,1)} %bitcast.65), calls=%async_computation.5 | async-start | bytes 1048576 | tf_op jit(solution)/shard_map/all_to_all | solution.py:95
  142.0 19.4 %collective-permute-start.15 = (bf16[256,512]{1,0:T(8,128)(2,1)}, bf16[256,512]{1,0:T(8,128)(2,1)}, u32[]{:S(2)}, u32[]{:S(2)}) collective-permute-start(bf16[256,512]{1,0:T(8,128)(2,1)} %bitcast.62), channel_id=1, source_target_pairs={{0,1},{1,0},{2,3},{3,2},{4,5},{5,4},{6,7},{7,6},{8,9},{9,8},{10,11... | collective-permute-start | bytes 786440 | tf_op jit(solution)/shard_map/ppermute | solution.py:22
  142.1 25.6 %collective-permute-start.17 = (bf16[256,512]{1,0:T(8,128)(2,1)S(1)}, bf16[256,512]{1,0:T(8,128)(2,1)}, u32[]{:S(2)}, u32[]{:S(2)}) collective-permute-start(bf16[256,512]{1,0:T(8,128)(2,1)S(1)} %bitcast.178), channel_id=1, source_target_pairs={{0,1},{1,0},{2,3},{3,2},{4,5},{5,4},{6,7},{7,6},{8,9},{9,8},{10,11... | collective-permute-start | bytes 786440 | tf_op jit(solution)/shard_map/ppermute | solution.py:22
  157.1 4.3 %collective-permute-start.16 = (bf16[256,1024]{1,0:T(8,128)(2,1)S(1)}, bf16[256,1024]{1,0:T(8,128)(2,1)S(1)}, u32[]{:S(2)}, u32[]{:S(2)}) collective-permute-start(bf16[256,1024]{1,0:T(8,128)(2,1)S(1)} %multiply_convert_fusion), channel_id=1, source_target_pairs={{0,1},{1,0},{2,3},{3,2},{4,5},{5,4},{6,7},{7,6},{8,9},{9,8},{10,11... | collective-permute-start | bytes 1572872 | tf_op jit(solution)/shard_map/ppermute | solution.py:22
  (23 other events, 171.0 us)
